TPU v7x, 32 devices: a whole 2x2x4 slice. The times are simulated.
32 devices in a mesh: base: 16 (over z, x, core), band: 2 (over y).
Axes of the slice: x: 2, y: 2, z: 4, core: 2. Of those that a mesh axis runs over, the one named last changes fastest.
Arguments:
- coherency: float32 [16, 16, 8, 4096], P('band', None, None, 'base'), may hold values from -1.5 to 1.5
- observed: float32 [16, 8, 4096], P('band', None, 'base'), may hold values from -6 to 6
- jones_deviation: float32 [16, 16, 8, 512], P('band', None, None, 'base'), may hold values from -1.8 to 1.8
- antenna_first: int32 [4096], P('base'), may hold values from 0 to 511, as said below
- antenna_second: int32 [4096], P('base'), may hold values from 0 to 511, as said below
Outputs:
- jones: float32 [16, 16, 8, 512], P('band', None, None, 'base')
- residual: float32 [16, 8, 4096], P('band', None, 'base')
Inputs may be any that keep to these rules, and one draw needn't show every extreme that they name: `antenna_first`: every station is the first station of exactly 8 baselines. On every baseline antenna_second differs from antenna_first.
All inputs are finite; a program needn't handle non-finite values.
Results may differ from a plain program's by a relative error of at most 0.0003.
Values sent between devices are 32-bit elements; how exact they have to be, the bound alone decides.
A program may use at most 128 MiB of HBM per device.

v0:
```python
import jax
import jax.numpy as jnp
from jax import lax
from jax.sharding import PartitionSpec as P

ITERS = 3


step_gain = 1.2
penalty_gain = 0.25


def expand_matrix(packed):
    return [
        [(packed[..., 0, :], packed[..., 1, :]), (packed[..., 2, :], packed[..., 3, :])],
        [(packed[..., 4, :], packed[..., 5, :]), (packed[..., 6, :], packed[..., 7, :])],
    ]


def pack_matrix(matrix):
    return jnp.stack(
        [
            matrix[0][0][0],
            matrix[0][0][1],
            matrix[0][1][0],
            matrix[0][1][1],
            matrix[1][0][0],
            matrix[1][0][1],
            matrix[1][1][0],
            matrix[1][1][1],
        ],
        axis=-2,
    )


def complex_mul(first_term, second_term):
    return (
        first_term[0] * second_term[0] - first_term[1] * second_term[1],
        first_term[0] * second_term[1] + first_term[1] * second_term[0],
    )


def complex_add(first_term, second_term):
    return (first_term[0] + second_term[0], first_term[1] + second_term[1])


def element_of(matrix, i, j, adjoint):
    if adjoint:
        return (matrix[j][i][0], -matrix[j][i][1])
    return matrix[i][j]


def matrix_product(first_factor, second_factor, adjoint_first=False, adjoint_second=False):
    result_rows = []
    for i in range(2):
        row_items = []
        for j in range(2):
            row_items.append(
                complex_add(
                    complex_mul(
                        element_of(first_factor, i, 0, adjoint_first),
                        element_of(second_factor, 0, j, adjoint_second),
                    ),
                    complex_mul(
                        element_of(first_factor, i, 1, adjoint_first),
                        element_of(second_factor, 1, j, adjoint_second),
                    ),
                )
            )
        result_rows.append(row_items)
    return result_rows


def fit_basis(band_count):
    positions = (2.0 * jnp.arange(band_count, dtype=jnp.float32) + 1.0) / band_count - 1.0
    columns = []
    for power in range(4):
        vector = positions**power
        for earlier in columns:
            vector = vector - jnp.sum(earlier * vector) * earlier
        vector = vector / jnp.sqrt(jnp.sum(vector * vector))
        columns.append(vector)
    return jnp.stack(columns, axis=1)


def local_gradients(
    leading_rows, trailing_rows, coherency, observed, antenna_first, antenna_second, station_number
):
    leading_jones = expand_matrix(leading_rows)
    trailing_jones = expand_matrix(trailing_rows)
    sky = expand_matrix(coherency)
    model = pack_matrix(
        matrix_product(leading_jones, matrix_product(sky, trailing_jones, adjoint_second=True))
    )
    residual = observed - jnp.sum(model, axis=1)
    resid_parts = expand_matrix(residual[:, None])
    gradient_leading = pack_matrix(
        matrix_product(resid_parts, matrix_product(trailing_jones, sky, adjoint_second=True))
    )
    gradient_trailing = pack_matrix(
        matrix_product(resid_parts, matrix_product(leading_jones, sky), adjoint_first=True)
    )
    shape_out = (coherency.shape[0], coherency.shape[1], 8, station_number)
    gradient_list = (
        jnp.zeros(shape_out, jnp.float32)
        .at[:, :, :, antenna_first]
        .add(gradient_leading)
        .at[:, :, :, antenna_second]
        .add(gradient_trailing)
    )
    return (gradient_list, residual)


def per_device(coherency, observed, jones_deviation, antenna_first, antenna_second):
    highest = lax.Precision.HIGHEST
    base_count = lax.axis_size("base")
    band_count = lax.axis_size("band")
    sub_dev = coherency.shape[0]
    base_dev = coherency.shape[-1]
    own_stations = jones_deviation.shape[-1]
    station_number = own_stations * base_count
    baseline_count = base_dev * base_count
    step_size = step_gain * station_number / baseline_count
    penalty = penalty_gain * baseline_count / station_number
    poly_basis = fit_basis(sub_dev * band_count)
    local_basis = lax.dynamic_slice_in_dim(poly_basis, lax.axis_index("band") * sub_dev, sub_dev, 0)
    identity = jnp.array([1.0, 0.0, 0.0, 0.0, 0.0, 0.0, 1.0, 0.0], dtype=jnp.float32)[:, None]
    jones_current = identity + jones_deviation
    jones_current = lax.all_gather(jones_current, "base", axis=3, tiled=True)
    consensus = jones_current
    dual_var = jnp.zeros_like(jones_current)
    residual = None
    for iteration in range(ITERS):
        leading_rows = jnp.take(jones_current, antenna_first, axis=3)
        trailing_rows = jnp.take(jones_current, antenna_second, axis=3)
        local_terms, residual = local_gradients(
            leading_rows,
            trailing_rows,
            coherency,
            observed,
            antenna_first,
            antenna_second,
            station_number,
        )
        station_gradients = lax.psum(local_terms, "base")
        jones_current = jones_current + step_size * (
            station_gradients - dual_var - penalty * (jones_current - consensus)
        )
        if iteration + 1 < ITERS:
            target = jones_current + dual_var / penalty
            partial_fit = jnp.einsum("fm,fkcs->mkcs", local_basis, target, precision=highest)
            coefficients = lax.psum(partial_fit, "band")
            consensus = jnp.einsum("fm,mkcs->fkcs", local_basis, coefficients, precision=highest)
            dual_var = dual_var + penalty * (jones_current - consensus)
    jones_current = lax.dynamic_slice_in_dim(
        jones_current, lax.axis_index("base") * own_stations, own_stations, 3
    )
    return (jones_current, residual)


def solution(mesh):
    return jax.shard_map(
        per_device,
        mesh=mesh,
        in_specs=(
            P("band", None, None, "base"),
            P("band", None, "base"),
            P("band", None, None, "base"),
            P("base"),
            P("base"),
        ),
        out_specs=(P("band", None, None, "base"), P("band", None, "base")),
        check_vma=False,
    )
```

profile of v0, /device:TPU:0, one launch (start us, length us, event | category | flops | bytes accessed | tf_op | source)
XLA Modules:
  0.0 1138.5 jit_solution(16276159739745969013)
XLA Ops:
  19.4 120.1 %all-gather.2.cloned.1.call-done = f32[8,16,8,512]{1,2,0,3:T(8,128)} async-done(((f32[8,16,8,32]{1,2,0,3:T(8,128)}), f32[8,16,8,512]{1,2,0,3:T(8,128)}) %all-gather.2.cloned.1.call-update) | async-done | bytes 2097168 | tf_op jit(solution)/shard_map/all_gather | solution.py:129
  139.5 11.4 copy.497
  150.9 10.6 gather_fusion
  168.6 10.6 gather_fusion.1
  239.8 8.0 copy.536
  254.8 39.9 %scatter_fusion = f32[8,16,8,512]{1,2,3,0:T(8,128)} fusion(f32[8,16,8,512]{1,2,3,0:T(8,128)} %broadcast.414.clone, s32[256]{0:T(256)S(1)} %copy-done.42, f32[256,8,16,8]{2,3,1,0:T(8,128)} %copy.527), kind=kCustom, calls=%fused_computation.6 | custom fusion | flops 262144 | bytes 3146752 | tf_op jit(solution)/shard_map/scatter-add | solution.py:107
  294.7 40.0 %scatter_fusion.1 = f32[8,16,8,512]{1,2,3,0:T(8,128)} fusion(f32[8,16,8,512]{1,2,3,0:T(8,128)} %scatter_fusion, s32[256]{0:T(256)S(1)} %copy-done.38, f32[256,8,16,8]{2,3,1,0:T(8,128)} %copy.536), kind=kCustom, calls=%fused_computation.7 | custom fusion | flops 262144 | bytes 3146752 | tf_op jit(solution)/shard_map/scatter-add | solution.py:109
  334.7 9.7 copy.537
  350.7 12.2 %copy.540 = f32[8,16,8,512]{3,0,2,1:T(8,128)} copy(f32[8,16,8,512]{1,2,0,3:T(8,128)} %all-gather.2.cloned.1.call-done) | data formatting | bytes 4194304 | tf_op jit(solution)/shard_map/all_gather | solution.py:129
  362.9 78.1 %all-reduce.6.cloned.1.call-done = f32[8,16,8,512]{3,0,2,1:T(8,128)} async-done(((f32[8,16,8,512]{3,0,2,1:T(8,128)}), f32[8,16,8,512]{3,0,2,1:T(8,128)}) %all-reduce.6.cloned.1.call-update) | async-done | bytes 2097168 | tf_op jit(solution)/shard_map/psum | solution.py:145
  451.6 10.8 gather_fusion.2
  462.4 10.8 gather_fusion.3
  586.1 39.9 %scatter_fusion.2 = f32[8,16,8,512]{1,2,3,0:T(8,128)} fusion(f32[8,16,8,512]{1,2,3,0:T(8,128)} %broadcast.414.clone.1, s32[256]{0:T(256)S(1)} %copy-done.43, f32[256,8,16,8]{2,3,1,0:T(8,128)} %copy.563), kind=kCustom, calls=%fused_computation.8 | custom fusion | flops 262144 | bytes 3146752 | tf_op jit(solution)/shard_map/scatter-add | solution.py:107
  625.9 39.7 %scatter_fusion.3 = f32[8,16,8,512]{1,2,3,0:T(8,128)} fusion(f32[8,16,8,512]{1,2,3,0:T(8,128)} %scatter_fusion.2, s32[256]{0:T(256)S(1)} %copy-done.39, f32[256,8,16,8]{2,3,1,0:T(8,128)} %copy.572), kind=kCustom, calls=%fused_computation.9 | custom fusion | flops 262144 | bytes 3146752 | tf_op jit(solution)/shard_map/scatter-add | solution.py:109
  665.7 9.7 copy.573
  686.6 86.5 %all-reduce.8.cloned.1.call-done = f32[8,16,8,512]{3,0,2,1:T(8,128)} async-done(((f32[8,16,8,512]{3,0,2,1:T(8,128)}), f32[8,16,8,512]{3,0,2,1:T(8,128)}) %all-reduce.8.cloned.1.call-update) | async-done | bytes 2097168 | tf_op jit(solution)/shard_map/psum | solution.py:145
  773.2 41.6 %all-reduce.10.cloned.1.call-done = f32[4,16,8,512]{3,0,2,1:T(4,128)} async-done(((f32[4,16,8,512]{3,0,2,1:T(4,128)}), f32[4,16,8,512]{3,0,2,1:T(4,128)}) %all-reduce.10.cloned.1.call-update) | async-done | bytes 1048592 | tf_op jit(solution)/shard_map/psum | solution.py:152
  828.5 10.8 gather_fusion.4
  839.3 10.8 gather_fusion.5
  912.6 8.4 copy.596
  940.5 39.9 %scatter_fusion.4 = f32[8,16,8,512]{1,2,3,0:T(8,128)} fusion(f32[8,16,8,512]{1,2,3,0:T(8,128)} %broadcast.414, s32[256]{0:T(256)S(1)} %copy-done.44, f32[256,8,16,8]{2,3,1,0:T(8,128)} %copy.596), kind=kCustom, calls=%fused_computation.10 | custom fusion | flops 262144 | bytes 3146752 | tf_op jit(solution)/shard_map/scatter-add | solution.py:107
  980.4 39.7 %scatter_fusion.5 = f32[8,16,8,512]{1,2,3,0:T(8,128)} fusion(f32[8,16,8,512]{1,2,3,0:T(8,128)} %scatter_fusion.4, s32[256]{0:T(256)S(1)} %copy-done.40, f32[256,8,16,8]{2,3,1,0:T(8,128)} %copy.605), kind=kCustom, calls=%fused_computation.11 | custom fusion | flops 262144 | bytes 3146752 | tf_op jit(solution)/shard_map/scatter-add | solution.py:109
  1020.2 10.0 copy.606
  1036.1 92.5 %all-reduce.12.cloned.1.call-done = f32[8,16,8,512]{3,0,2,1:T(8,128)} async-done(((f32[8,16,8,512]{3,0,2,1:T(8,128)}), f32[8,16,8,512]{3,0,2,1:T(8,128)}) %all-reduce.12.cloned.1.call-update) | async-done | bytes 2097168 | tf_op jit(solution)/shard_map/psum | solution.py:145
  (313 shorter events, 327.6 us)
Async XLA Ops:
  7.2 132.3 %all-gather.2.cloned.1.call-start = ((), (), s32[]{:S(2)}) async-start(), calls=%async_computation | async-start | bytes 17825792 | tf_op jit(solution)/shard_map/all_gather | solution.py:129
  10.2 430.8 %all-reduce.6.cloned.1.call-start = ((), (), s32[]{:S(2)}) async-start(), calls=%async_computation.1 | async-start | bytes 4194304 | tf_op jit(solution)/shard_map/psum | solution.py:145
  11.5 187.0 %copy-start.13 = (f32[8,8,256]{1,0,2:T(8,128)}, f32[8,8,256]{1,0,2:T(8,128)S(1)}, u32[]{:S(2)}) copy-start(f32[8,8,256]{1,0,2:T(8,128)S(1)} %copy.510) | copy-start | bytes 196612
  12.3 138.6 %copy-start.45 = (s32[1024]{0:T(1024)}, s32[1024]{0:T(1024)S(1)}, u32[]{:S(2)}) copy-start(s32[1024]{0:T(1024)S(1)} %pad_clamp_fusion.1) | copy-start | bytes 12292
  12.9 155.8 %copy-start.46 = (s32[1024]{0:T(1024)}, s32[1024]{0:T(1024)S(1)}, u32[]{:S(2)}) copy-start(s32[1024]{0:T(1024)S(1)} %pad_clamp_fusion) | copy-start | bytes 12292
  13.6 173.0 %copy-start.50 = (pred[256]{0:T(512)(128)(4,1)}, pred[256]{0:T(512)(128)(4,1)S(1)}, u32[]{:S(2)}) copy-start(pred[256]{0:T(512)(128)(4,1)S(1)} %get-tuple-element.206) | copy-start | bytes 772
  13.6 174.4 %copy-start.47 = (pred[256]{0:T(512)(128)(4,1)}, pred[256]{0:T(512)(128)(4,1)S(1)}, u32[]{:S(2)}) copy-start(pred[256]{0:T(512)(128)(4,1)S(1)} %get-tuple-element.205) | copy-start | bytes 772
  19.3 198.0 %copy-start.5 = (f32[8,16,1,256]{3,2,1,0:T(1,128)}, f32[8,16,1,256]{3,2,1,0:T(1,128)S(1)}, u32[]{:S(2)}) copy-start(f32[8,16,1,256]{3,2,1,0:T(1,128)S(1)} %get-tuple-element.140) | copy-start | bytes 393220
  19.3 198.0 %copy-start.7 = (f32[8,16,1,256]{3,2,1,0:T(1,128)}, f32[8,16,1,256]{3,2,1,0:T(1,128)S(1)}, u32[]{:S(2)}) copy-start(f32[8,16,1,256]{3,2,1,0:T(1,128)S(1)} %get-tuple-element.142) | copy-start | bytes 393220
  19.4 198.0 %copy-start.9 = (f32[8,16,1,256]{3,2,1,0:T(1,128)}, f32[8,16,1,256]{3,2,1,0:T(1,128)S(1)}, u32[]{:S(2)}) copy-start(f32[8,16,1,256]{3,2,1,0:T(1,128)S(1)} %get-tuple-element.145) | copy-start | bytes 393220
  19.4 198.0 %copy-start.11 = (f32[8,16,1,256]{3,2,1,0:T(1,128)}, f32[8,16,1,256]{3,2,1,0:T(1,128)S(1)}, u32[]{:S(2)}) copy-start(f32[8,16,1,256]{3,2,1,0:T(1,128)S(1)} %get-tuple-element.146) | copy-start | bytes 393220
  19.4 199.5 %copy-start.3 = (f32[8,16,1,256]{3,2,1,0:T(1,128)}, f32[8,16,1,256]{3,2,1,0:T(1,128)S(1)}, u32[]{:S(2)}) copy-start(f32[8,16,1,256]{3,2,1,0:T(1,128)S(1)} %get-tuple-element.147) | copy-start | bytes 393220
  247.7 47.0 %copy-start.38 = (s32[256]{0:T(256)S(1)}, s32[256]{0:T(256)}, u32[]{:S(2)}) copy-start(s32[256]{0:T(256)} %copy-done.37) | copy-start | bytes 3076
  344.4 428.7 %all-reduce.8.cloned.1.call-start = ((), (), s32[]{:S(2)}) async-start(), calls=%async_computation.2 | async-start | bytes 4194304 | tf_op jit(solution)/shard_map/psum | solution.py:145
  443.9 239.9 %copy-start.2 = (f32[8,16,8,512]{3,0,2,1:T(8,128)}, f32[8,16,8,512]{3,0,2,1:T(8,128)S(1)}, u32[]{:S(2)}) copy-start(f32[8,16,8,512]{3,0,2,1:T(8,128)S(1)} %multiply_add_fusion) | copy-start | bytes 6291460
  451.6 28.7 %copy-start.51 = (pred[256]{0:T(512)(128)(4,1)S(1)}, pred[256]{0:T(512)(128)(4,1)}, u32[]{:S(2)}) copy-start(pred[256]{0:T(512)(128)(4,1)} %copy-done.50) | copy-start | bytes 772
  473.2 15.8 %copy-start.48 = (pred[256]{0:T(512)(128)(4,1)S(1)}, pred[256]{0:T(512)(128)(4,1)}, u32[]{:S(2)}) copy-start(pred[256]{0:T(512)(128)(4,1)} %copy-done.47) | copy-start | bytes 772
  579.0 47.0 %copy-start.39 = (s32[256]{0:T(256)S(1)}, s32[256]{0:T(256)}, u32[]{:S(2)}) copy-start(s32[256]{0:T(256)} %copy-done.37) | copy-start | bytes 3076
  675.4 139.3 %all-reduce.10.cloned.1.call-start = ((), (), s32[]{:S(2)}) async-start(), calls=%async_computation.3 | async-start | bytes 2097152 | tf_op jit(solution)/shard_map/psum | solution.py:152
  683.7 144.8 %copy-start.35 = (f32[16,4]{0,1:T(4,128)}, f32[16,4]{0,1:T(4,128)S(1)}, u32[]{:S(2)}) copy-start(f32[16,4]{0,1:T(4,128)S(1)} %pad_maximum_fusion) | copy-start | bytes 772
  686.6 344.6 %all-reduce.14.cloned.1.call-start = ((), (), s32[]{:S(2)}) async-start(), calls=%async_computation.5 | async-start | bytes 2097152 | tf_op jit(solution)/shard_map/psum | solution.py:152
  828.5 27.8 %copy-start.52 = (pred[256]{0:T(512)(128)(4,1)S(1)}, pred[256]{0:T(512)(128)(4,1)}, u32[]{:S(2)}) copy-start(pred[256]{0:T(512)(128)(4,1)} %copy-done.50) | copy-start | bytes 772
  900.7 227.8 %all-reduce.12.cloned.1.call-start = ((), (), s32[]{:S(2)}) async-start(), calls=%async_computation.4 | async-start | bytes 4194304 | tf_op jit(solution)/shard_map/psum | solution.py:145
  933.4 47.0 %copy-start.40 = (s32[256]{0:T(256)S(1)}, s32[256]{0:T(256)}, u32[]{:S(2)}) copy-start(s32[256]{0:T(256)} %copy-done.37) | copy-start | bytes 3076
  (36 other events, 244.9 us)
Sparse Core Ops, SparseCore 0:
  10.3 129.1 all-gather.1
  344.5 96.3 all-reduce.5
  675.5 97.6 all-reduce.7
  775.3 39.3 all-reduce.9
  900.9 40.0 all-reduce.13
  1030.3 98.1 all-reduce.11
where the time goes:
time: 1150 us; the launch traced here: 1140 us
  waiting for transfers between devices  419 us (36%)
  local copies, waits for them, and re-layouts  357 us (31%)
  other arithmetic  325 us (28%)
  between operations  19.3 us (2%)
  matrix products  18.8 us (2%)
    psum x3, waiting for transfers between devices, per_device(): station_gradients = lax.psum(local_terms, 'base')  257 us
    scatter-add x6, other arithmetic, local_gradients(): gradient_list = jnp.zeros(shape_out, jnp.float32).at[:, :, :, antenna_fir...  239 us
    all_gather x1, waiting for transfers between devices, per_device(): jones_current = lax.all_gather(jones_current, 'base', axis=3, tiled=True)  120 us
    another operation x12, local copies, waits for them, and re-layouts, pack_matrix(): jnp.stack([matrix[0][0][0], matrix[0][0][1], matrix[0][1][0], matrix[0][1...  61.3 us
    gather x6, local copies, waits for them, and re-layouts, per_device(): trailing_rows = jnp.take(jones_current, antenna_second, axis=3)  53.5 us
    gather x6, local copies, waits for them, and re-layouts, per_device(): leading_rows = jnp.take(jones_current, antenna_first, axis=3)  52.7 us
    psum x2, waiting for transfers between devices, per_device(): coefficients = lax.psum(partial_fit, 'band')  41.6 us
    scatter-add x3, local copies, waits for them, and re-layouts, local_gradients(): gradient_list = jnp.zeros(shape_out, jnp.float32).at[:, :, :, antenna_fir...  29.4 us
  transfers between devices with their start and end apart: 6, of which 5 were waited for; matrix products, arithmetic and copies ran while one was open for 15% of the time, Pallas kernels for 0%

commit v1 on v0

v1 whole, which is shorter than its diff:
```python
import functools

import jax
import jax.numpy as jnp
import numpy as np
from jax import lax
from jax.experimental import pallas as pl
from jax.experimental.pallas import tpu as pltpu
from jax.sharding import PartitionSpec as P

ITERS = 3
STEP_GAIN = 1.2
PENALTY_GAIN = 0.25
MESH = pl.DeviceIdType.MESH
HIGHEST = lax.Precision.HIGHEST


def fit_basis(band_count):
    positions = ((2.0 * np.arange(band_count) + 1.0) / band_count - 1.0).astype(np.float64)
    columns = []
    for power in range(4):
        vector = positions**power
        for earlier in columns:
            vector = vector - np.sum(earlier * vector) * earlier
        columns.append(vector / np.sqrt(np.sum(vector * vector)))
    return np.stack(columns, axis=1)


def components(x):
    n = x.shape[0] // 8
    c = [x[i * n : (i + 1) * n] for i in range(8)]
    return [[(c[0], c[1]), (c[2], c[3])], [(c[4], c[5]), (c[6], c[7])]]


def flat(m):
    return [m[i][j][p] for i in range(2) for j in range(2) for p in range(2)]


def cmul(a, b):
    return (a[0] * b[0] - a[1] * b[1], a[0] * b[1] + a[1] * b[0])


def element_of(m, i, j, adjoint):
    return (m[j][i][0], -m[j][i][1]) if adjoint else m[i][j]


def product(a, b, adjoint_a=False, adjoint_b=False):
    rows = []
    for i in range(2):
        row = []
        for j in range(2):
            u = cmul(element_of(a, i, 0, adjoint_a), element_of(b, 0, j, adjoint_b))
            v = cmul(element_of(a, i, 1, adjoint_a), element_of(b, 1, j, adjoint_b))
            row.append((u[0] + v[0], u[1] + v[1]))
        rows.append(row)
    return rows


def split_rows(x):
    high = x.astype(jnp.bfloat16)
    low = (x - high.astype(jnp.float32)).astype(jnp.bfloat16)
    return jnp.concatenate([high, low], axis=0)


def wait_bytes(ref, sem):
    pltpu.make_async_copy(ref, ref, sem).wait()


def kernel(
    cfg,
    coh, obs, dev, first, second,
    out_j, out_r,
    first_v, second_v, dev_v, obs_v, coh_v,
    onehot, cohc, left_t, right_t, model, model_r,
    jj, jones, dual, cons, acc,
    t_send, t_recv, z_send, z_recv, res, j_send,
    in_send, in_recv, coh_send, coh_recv,
    m_send, m_recv, ts_sem, tr_sem, zs_sem, zr_sem, o_send, o_recv,
):
    nb, nband, F, g, K, Kg, So, S, Bo, step, penalty, npc, lane_parts, groups = cfg
    rows = 8 * Kg
    N = F * nband
    L = S // lane_parts
    basis = fit_basis(N)
    me = lax.axis_index("base")
    mb = lax.axis_index("band")
    s = me // g
    r = me % g
    mine = mb * F + s
    cg = nb // groups

    barrier = pltpu.get_barrier_semaphore()

    def greet(o, _):
        pl.semaphore_signal(barrier, inc=1, device_id={"base": (me + o) % nb}, device_id_type=MESH)
        return 0

    lax.fori_loop(1, nb, greet, 0)
    for ob in range(1, nband):
        def greet_band(f, _):
            pl.semaphore_signal(
                barrier, inc=1,
                device_id={"band": (mb + ob) % nband, "base": f * g + r}, device_id_type=MESH,
            )
            return 0

        lax.fori_loop(0, F, greet_band, 0)
    pl.semaphore_wait(barrier, nb - 1 + F * (nband - 1))

    def small(kind, d):
        f = d // g
        k0 = (d % g) * Kg
        return [
            (first, first_v.at[me]),
            (second, second_v.at[me]),
            (dev.at[f, pl.ds(k0, Kg)], dev_v.at[me]),
            (obs.at[f], obs_v.at[me]),
        ][kind]

    for kind in range(4):
        def send_small(o, _):
            d = (me + o) % nb
            src, dst = small(kind, d)
            pltpu.make_async_remote_copy(
                src, dst, in_send.at[kind], in_recv.at[kind],
                device_id={"base": d}, device_id_type=MESH,
            ).start()
            return 0

        src, dst = small(kind, me)
        pltpu.make_async_copy(src, dst, in_recv.at[kind]).start()
        lax.fori_loop(1, nb, send_small, 0)

    def coh_block(d):
        return coh.at[d // g, pl.ds((d % g) * Kg, Kg)]

    pltpu.make_async_copy(coh_block(me), coh_v.at[me], coh_recv.at[me]).start()

    def send_coh(o, _):
        d = (me + o) % nb
        pltpu.make_async_remote_copy(
            coh_block(d), coh_v.at[me], coh_send, coh_recv.at[me],
            device_id={"base": d}, device_id_type=MESH,
        ).start()
        return 0

    lax.fori_loop(1, nb, send_coh, 0)

    wait_bytes(first_v, in_recv.at[0])
    wait_bytes(second_v, in_recv.at[1])

    def build(i, _):
        at = lax.broadcasted_iota(jnp.int32, (S, Bo), 0)
        onehot[i, :, 0:Bo] = jnp.where(at == first_v[i], 1.0, 0.0).astype(jnp.bfloat16)
        onehot[i, :, Bo : 2 * Bo] = jnp.where(at == second_v[i], 1.0, 0.0).astype(jnp.bfloat16)
        return 0

    lax.fori_loop(0, nb, build, 0)

    row = lax.broadcasted_iota(jnp.int32, (rows, rows), 0)
    col = lax.broadcasted_iota(jnp.int32, (rows, rows), 1)
    to_major = jnp.where(col == (row % Kg) * 8 + row // Kg, 1.0, 0.0)
    from_major = jnp.where(col == (row % 8) * Kg + row // 8, 1.0, 0.0)

    wait_bytes(dev_v, in_recv.at[2])
    for i in range(nb):
        acc[0:rows, i * So : (i + 1) * So] = dev_v[i].reshape(rows, So)
    start = jnp.dot(to_major, acc[0:rows], precision=HIGHEST, preferred_element_type=jnp.float32)
    which = lax.broadcasted_iota(jnp.int32, (rows, S), 0) // Kg
    jones[...] = start + jnp.where((which == 0) | (which == 6), 1.0, 0.0)
    wait_bytes(obs_v, in_recv.at[3])

    def owner(j):
        return {"band": j // F, "base": (j % F) * g + r}

    def t_copy(t, j):
        return pltpu.make_async_remote_copy(
            t_send.at[t, j], t_recv.at[t, mine], ts_sem.at[t, j], tr_sem.at[t, mine],
            device_id=owner(j), device_id_type=MESH,
        )

    def z_copy(t, f):
        return pltpu.make_async_remote_copy(
            z_send.at[t, f], z_recv.at[t, mine], zs_sem.at[t, f], zr_sem.at[t, mine],
            device_id=owner(f), device_id_type=MESH,
        )

    for t in range(ITERS):
        jj[...] = split_rows(jones[...])

        def send_models(q):
            for o in range(1, g):
                d = (r + o) % g
                pltpu.make_async_remote_copy(
                    model.at[t, pl.ds(q * cg, cg)], model_r.at[t, o - 1, pl.ds(q * cg, cg)],
                    m_send, m_recv.at[t, o - 1, q],
                    device_id={"base": s * g + d}, device_id_type=MESH,
                ).start()

        def forward(i, _):
            if t == 0:
                wait_bytes(coh_v.at[i], coh_recv.at[i])
                sky_rows = jnp.dot(
                    to_major, coh_v[i].reshape(rows, Bo), precision=HIGHEST,
                    preferred_element_type=jnp.float32,
                )
                cohc[i] = sky_rows
            else:
                sky_rows = cohc[i]
            both = jnp.dot(jj[...], onehot[i], preferred_element_type=jnp.float32)
            both = both[0:rows] + both[rows:]
            sky = components(sky_rows)
            leading = components(both[:, 0:Bo])
            trailing = components(both[:, Bo:])
            m = product(sky, trailing, adjoint_b=True)
            a = product(leading, sky)
            v = product(leading, m)
            left_t[i] = jnp.concatenate(flat(m), axis=0)
            right_t[i] = jnp.concatenate(flat(a), axis=0)
            model[t, i] = jnp.concatenate(
                [jnp.sum(x, axis=0, keepdims=True) for x in flat(v)], axis=0
            )
            return 0

        for q in range(groups):
            lax.fori_loop(q * cg, (q + 1) * cg, forward, 0)
            send_models(q)

        if t > 0:
            u = t - 1

            @pl.when(mine < npc)
            def _():
                for f in range(N):
                    wait_bytes(t_recv.at[u, f], tr_sem.at[u, f])
                coefficients = []
                for m in range(4):
                    total = float(basis[0, m]) * t_recv[u, 0]
                    for f in range(1, N):
                        total = total + float(basis[f, m]) * t_recv[u, f]
                    coefficients.append(total)
                for f in range(N):
                    value = float(basis[f, 0]) * coefficients[0]
                    for m in range(1, 4):
                        value = value + float(basis[f, m]) * coefficients[m]
                    z_send[u, f] = value
                for f in range(N):
                    @pl.when(mine != f)
                    def _():
                        z_copy(u, f).start()

                    @pl.when(mine == f)
                    def _():
                        pltpu.make_async_copy(z_send.at[u, f], z_recv.at[u, f], zr_sem.at[u, f]).start()

        acc[...] = jnp.zeros_like(acc)

        def backward(i, _):
            total = model[t, i]
            for o in range(1, g):
                total = total + model_r[t, o - 1, i]
            value = obs_v[i] - total
            if t == ITERS - 1:
                res[i] = value
            resid = components(value)
            gl = product(resid, components(left_t[i]), adjoint_b=True)
            gt = product(resid, components(right_t[i]), adjoint_a=True)
            both = jnp.concatenate(
                [jnp.concatenate(flat(gl), axis=0), jnp.concatenate(flat(gt), axis=0)], axis=1
            )
            acc[...] += lax.dot_general(
                split_rows(both), onehot[i], (((1,), (1,)), ((), ())),
                preferred_element_type=jnp.float32,
            )
            return 0

        for q in range(groups):
            for o in range(1, g):
                wait_bytes(model_r.at[t, o - 1, pl.ds(q * cg, cg)], m_recv.at[t, o - 1, q])
            lax.fori_loop(q * cg, (q + 1) * cg, backward, 0)

        if t == ITERS - 1:
            def send_res(f, _):
                d = f * g + r

                @pl.when(f != s)
                def _():
                    pltpu.make_async_remote_copy(
                        res.at[d], out_r.at[s], o_send.at[0], o_recv.at[0],
                        device_id={"base": d}, device_id_type=MESH,
                    ).start()

                @pl.when(f == s)
                def _():
                    pltpu.make_async_copy(res.at[d], out_r.at[s], o_recv.at[0]).start()

                return 0

            lax.fori_loop(0, F, send_res, 0)

        gradient = acc[0:rows] + acc[rows:]
        current = jones[...]
        if t == 0:
            updated = current + step * gradient
            target = updated
        else:
            u = t - 1
            for j in range(npc):
                wait_bytes(z_recv.at[u, j], zr_sem.at[u, j])
                r0, l0 = (j // lane_parts) * 8, (j % lane_parts) * L
                cons[r0 : r0 + 8, l0 : l0 + L] = z_recv[u, j]
            dual_var = penalty * (current - cons[...])
            if t > 1:
                dual_var = dual_var + dual[...]
            if t < ITERS - 1:
                dual[...] = dual_var
            updated = current + step * (gradient - dual_var - penalty * (current - cons[...]))
            target = updated + dual_var / penalty
        jones[...] = updated
        if t < ITERS - 1:
            for j in range(npc):
                r0, l0 = (j // lane_parts) * 8, (j % lane_parts) * L
                t_send[t, j] = target[r0 : r0 + 8, l0 : l0 + L]
            for j in range(npc):
                @pl.when(mine != j)
                def _():
                    t_copy(t, j).start()

                @pl.when(mine == j)
                def _():
                    pltpu.make_async_copy(t_send.at[t, j], t_recv.at[t, j], tr_sem.at[t, j]).start()

    final = jnp.dot(from_major, jones[...], precision=HIGHEST, preferred_element_type=jnp.float32)
    for d in range(nb):
        j_send[d] = final[:, d * So : (d + 1) * So].reshape(Kg, 8, So)
    place = out_j.at[s, pl.ds(r * Kg, Kg)]
    pltpu.make_async_copy(j_send.at[me], place, o_recv.at[1]).start()

    def send_jones(o, _):
        d = (me + o) % nb
        pltpu.make_async_remote_copy(
            j_send.at[d], place, o_send.at[1], o_recv.at[1],
            device_id={"base": d}, device_id_type=MESH,
        ).start()
        return 0

    lax.fori_loop(1, nb, send_jones, 0)

    for kind, buffer in enumerate([first_v, second_v, dev_v, obs_v]):
        wait_bytes(buffer.at[pl.ds(0, nb - 1)], in_send.at[kind])
    wait_bytes(coh_v.at[pl.ds(0, nb - 1)], coh_send)
    if g > 1:
        wait_bytes(model_r, m_send)
    for t in range(ITERS - 1):
        for j in range(npc):
            @pl.when(mine != j)
            def _():
                t_copy(t, j).wait_send()

        @pl.when(mine < npc)
        def _():
            for f in range(N):
                @pl.when(mine != f)
                def _():
                    z_copy(t, f).wait_send()
    wait_bytes(res.at[pl.ds(0, F - 1)], o_send.at[0])
    wait_bytes(j_send.at[pl.ds(0, nb - 1)], o_send.at[1])
    wait_bytes(out_r, o_recv.at[0])
    wait_bytes(j_send, o_recv.at[1])


def per_device(coherency, observed, jones_deviation, antenna_first, antenna_second):
    nb = lax.axis_size("base")
    nband = lax.axis_size("band")
    F, K, _, Bo = coherency.shape
    So = jones_deviation.shape[-1]
    S, B = So * nb, Bo * nb
    g = nb // F
    Kg = K // g
    rows = 8 * Kg
    N = F * nband
    step = STEP_GAIN * S / B
    penalty = PENALTY_GAIN * B / S
    lane_tiles = S // 128
    lane_parts = lane_tiles
    while lane_parts % 2 == 0 and Kg * lane_parts > N:
        lane_parts //= 2
    npc = Kg * lane_parts
    L = S // lane_parts
    groups = 4
    gp = max(g - 1, 1)
    cfg = (nb, nband, F, g, K, Kg, So, S, Bo, step, penalty, npc, lane_parts, groups)
    f32, bf16, i32 = jnp.float32, jnp.bfloat16, jnp.int32
    V, D = pltpu.VMEM, pltpu.SemaphoreType.DMA
    anywhere = pl.BlockSpec(memory_space=pl.ANY)
    return tuple(
        pl.pallas_call(
            functools.partial(kernel, cfg),
            out_shape=(
                jax.ShapeDtypeStruct((F, K, 8, So), f32),
                jax.ShapeDtypeStruct((F, 8, Bo), f32),
            ),
            in_specs=[anywhere] * 5,
            out_specs=(anywhere, anywhere),
            scratch_shapes=[
                V((nb, 1, Bo), i32),
                V((nb, 1, Bo), i32),
                V((nb, Kg, 8, So), f32),
                V((nb, 8, Bo), f32),
                V((nb, Kg, 8, Bo), f32),
                V((nb, S, 2 * Bo), bf16),
                V((nb, rows, Bo), f32),
                V((nb, rows, Bo), f32),
                V((nb, rows, Bo), f32),
                V((ITERS, nb, 8, Bo), f32),
                V((ITERS, gp, nb, 8, Bo), f32),
                V((2 * rows, S), bf16),
                V((rows, S), f32),
                V((rows, S), f32),
                V((rows, S), f32),
                V((2 * rows, S), f32),
                V((ITERS - 1, npc, 8, L), f32),
                V((ITERS - 1, N, 8, L), f32),
                V((ITERS - 1, N, 8, L), f32),
                V((ITERS - 1, npc, 8, L), f32),
                V((nb, 8, Bo), f32),
                V((nb, Kg, 8, So), f32),
                D((4,)),
                D((4,)),
                D,
                D((nb,)),
                D,
                D((ITERS, gp, groups)),
                D((ITERS - 1, npc)),
                D((ITERS - 1, N)),
                D((ITERS - 1, N)),
                D((ITERS - 1, npc)),
                D((2,)),
                D((2,)),
            ],
            compiler_params=pltpu.CompilerParams(
                collective_id=0, has_side_effects=True, vmem_limit_bytes=60 * 1024 * 1024
            ),
        )(
            coherency, observed, jones_deviation,
            antenna_first.reshape(1, Bo), antenna_second.reshape(1, Bo),
        )
    )


def solution(mesh):
    return jax.shard_map(
        per_device,
        mesh=mesh,
        in_specs=(
            P("band", None, None, "base"),
            P("band", None, "base"),
            P("band", None, None, "base"),
            P("base"),
            P("base"),
        ),
        out_specs=(P("band", None, None, "base"), P("band", None, "base")),
        check_vma=False,
    )
```

time: 1150 us -> 91.9 us (0.08)
  waiting for transfers between devices: 419 us -> 0 us
  local copies, waits for them, and re-layouts: 357 us -> 2.54 us
  other arithmetic: 325 us -> 0 us
  Pallas kernels: 0 us -> 88.2 us
  matrix products: 18.8 us -> 0 us
  between operations: 19.3 us -> 0.65 us
    psum x5 -> x0, waiting for transfers between devices: 299 us -> none  [the longest x3 257 us: per_device(): station_gradients = lax.psum(local_terms, 'base')]
    scatter-add x6 -> x0, other arithmetic: 239 us -> none  [local_gradients(): gradient_list = jnp.zeros(shape_out, jnp.float32).at[:, :, :, antenna_fir...]
    all_gather x1 -> x0, waiting for transfers between devices: 120 us -> none  [per_device(): jones_current = lax.all_gather(jones_current, 'base', axis=3, tiled=True)]
    gather x12 -> x0, local copies, waits for them, and re-layouts: 106 us -> none  [the longest x6 53.5 us: per_device(): trailing_rows = jnp.take(jones_current, antenna_second, axis=3)]
    pallas_call x0 -> x1, Pallas kernels: none -> 88.2 us  [per_device(): pl.pallas_call(functools.partial(kernel, cfg), out_shape=(jax.ShapeDtypeS...]
    another operation x16 -> x0, local copies, waits for them, and re-layouts: 82.6 us -> none  [the longest x12 61.3 us: pack_matrix(): jnp.stack([matrix[0][0][0], matrix[0][0][1], matrix[0][1][0], matrix[0][1...]
    slice x28 -> x0, local copies, waits for them, and re-layouts: 62.2 us -> none  [the longest x6 19.7 us: expand_matrix(): packed[..., 0, :]]
    add x51 -> x0, local copies, waits for them, and re-layouts: 42.8 us -> none  [the longest x48 25.4 us: complex_add(): return (first_term[0] + second_term[0], first_term[1] + second_term[1])]
  transfers between devices with their start and end apart: 6 -> 0, of which waited for: 5 -> 0; matrix products, arithmetic and copies ran while one was open for 15% -> 0% of each run, Pallas kernels for 0% -> 0%
where the time goes in v1:
time: 91.9 us; the launch traced here: 91.3 us
  Pallas kernels  88.2 us (96%)
  local copies, waits for them, and re-layouts  2.54 us (3%)
    pallas_call x1, Pallas kernels, per_device(): pl.pallas_call(functools.partial(kernel, cfg), out_shape=(jax.ShapeDtypeS...  88.2 us
    unnamed x4, local copies, waits for them, and re-layouts  2.54 us

profile of v1, /device:TPU:0, one launch (start us, length us, event | category | flops | bytes accessed | tf_op | source)
XLA Modules:
  0.0 91.3 jit_solution(11421378623024218032)
XLA Ops:
  0.6 88.2 %shard_map.68 = (f32[8,16,8,32]{3,2,1,0:T(8,128)}, f32[8,8,256]{2,1,0:T(8,128)}) custom-call(f32[8,16,8,256]{3,2,1,0:T(8,128)} %coh.1, f32[8,8,256]{2,1,0:T(8,128)} %obs.1, f32[8,16,8,32]{3,2,1,0:T(8,128)} %dev.1, s32[1,256]{1,0:T(1,128)} %bitcast.2, s32[1,256]{1,0:T(1,128)} %bitcast.3), custom_call_target="tpu_custom_call" | custom-call | tf_op jit(solution)/shard_map/pallas_call | solution.py:397
  88.8 0.0 copy-start
  88.8 1.9 %copy.9 = f32[8,16,8,32]{3,2,1,0:T(8,128)} copy(f32[8,16,8,32]{3,2,1,0:T(8,128)} %get-tuple-element.4) | data formatting | bytes 262144
  90.7 0.0 copy-done
  90.7 0.6 copy.10
Async XLA Ops:
  88.8 1.9 %copy-start = (f32[8,8,256]{2,1,0:T(8,128)S(1)}, f32[8,8,256]{2,1,0:T(8,128)}, u32[]{:S(2)}) copy-start(f32[8,8,256]{2,1,0:T(8,128)} %get-tuple-element.5) | copy-start | bytes 196612

commit v2 on v1

--- a/solution.py
+++ b/solution.py
@@ -66,19 +66,30 @@
     pltpu.make_async_copy(ref, ref, sem).wait()
 
 
+def unpack_kernel(cfg, packed, residual_in, jones, residual):
+    nb, g, Kg, So, fold = cfg
+    k = Kg // fold
+    for i in range(nb):
+        for q in range(fold):
+            at = (i % g) * Kg + q * k
+            jones[i // g, at : at + k] = packed[i, :, q * So : (q + 1) * So].reshape(k, 8, So)
+    residual[...] = residual_in[...]
+
+
 def kernel(
     cfg,
     coh, obs, dev, first, second,
-    out_j, out_r,
-    first_v, second_v, dev_v, obs_v, coh_v,
+    out_p, out_r,
+    dev_in, dev_s, first_v, second_v, dev_v, obs_v, coh_v,
     onehot, cohc, left_t, right_t, model, model_r,
     jj, jones, dual, cons, acc,
     t_send, t_recv, z_send, z_recv, res, j_send,
-    in_send, in_recv, coh_send, coh_recv,
+    dev_sem, in_send, in_recv, coh_send, coh_recv,
     m_send, m_recv, ts_sem, tr_sem, zs_sem, zr_sem, o_send, o_recv,
 ):
-    nb, nband, F, g, K, Kg, So, S, Bo, step, penalty, npc, lane_parts, groups = cfg
+    nb, nband, F, g, K, Kg, So, S, Bo, step, penalty, npc, lane_parts, groups, fold = cfg
     rows = 8 * Kg
+    short = rows // fold
     N = F * nband
     L = S // lane_parts
     basis = fit_basis(N)
@@ -88,6 +99,14 @@
     r = me % g
     mine = mb * F + s
     cg = nb // groups
+    load_dev = pltpu.make_async_copy(dev, dev_in, dev_sem)
+    load_dev.start()
+
+    def chunk(p):
+        return ((s - p // g + F) % F) * g + p % g
+
+    def target_of(o):
+        return ((s + o // g) % F) * g + (r + o) % g
 
     barrier = pltpu.get_barrier_semaphore()
 
@@ -113,11 +132,22 @@
         return [
             (first, first_v.at[me]),
             (second, second_v.at[me]),
-            (dev.at[f, pl.ds(k0, Kg)], dev_v.at[me]),
+            (dev_s.at[d], dev_v.at[me]),
             (obs.at[f], obs_v.at[me]),
         ][kind]
 
-    for kind in range(4):
+    for kind in (0, 1, 3, 2):
+        if kind == 2:
+            load_dev.wait()
+
+            def fold_block(d, _):
+                block = dev_in[d // g, pl.ds((d % g) * Kg, Kg)].reshape(rows, So)
+                for q in range(fold):
+                    dev_s[d, :, q * So : (q + 1) * So] = block[q * short : (q + 1) * short]
+                return 0
+
+            lax.fori_loop(0, nb, fold_block, 0)
+
         def send_small(o, _):
             d = (me + o) % nb
             src, dst = small(kind, d)
@@ -137,7 +167,7 @@
     pltpu.make_async_copy(coh_block(me), coh_v.at[me], coh_recv.at[me]).start()
 
     def send_coh(o, _):
-        d = (me + o) % nb
+        d = target_of(o)
         pltpu.make_async_remote_copy(
             coh_block(d), coh_v.at[me], coh_send, coh_recv.at[me],
             device_id={"base": d}, device_id_type=MESH,
@@ -164,7 +194,10 @@
 
     wait_bytes(dev_v, in_recv.at[2])
     for i in range(nb):
-        acc[0:rows, i * So : (i + 1) * So] = dev_v[i].reshape(rows, So)
+        for q in range(fold):
+            acc[q * short : (q + 1) * short, i * So : (i + 1) * So] = dev_v[
+                i, :, q * So : (q + 1) * So
+            ]
     start = jnp.dot(to_major, acc[0:rows], precision=HIGHEST, preferred_element_type=jnp.float32)
     which = lax.broadcasted_iota(jnp.int32, (rows, S), 0) // Kg
     jones[...] = start + jnp.where((which == 0) | (which == 6), 1.0, 0.0)
@@ -197,7 +230,8 @@
                     device_id={"base": s * g + d}, device_id_type=MESH,
                 ).start()
 
-        def forward(i, _):
+        def forward(p, _):
+            i = chunk(p)
             if t == 0:
                 wait_bytes(coh_v.at[i], coh_recv.at[i])
                 sky_rows = jnp.dot(
@@ -217,14 +251,43 @@
             v = product(leading, m)
             left_t[i] = jnp.concatenate(flat(m), axis=0)
             right_t[i] = jnp.concatenate(flat(a), axis=0)
-            model[t, i] = jnp.concatenate(
+            model[t, p] = jnp.concatenate(
                 [jnp.sum(x, axis=0, keepdims=True) for x in flat(v)], axis=0
             )
             return 0
 
+        acc[...] = jnp.zeros_like(acc)
+
+        def backward(p, _):
+            i = chunk(p)
+            total = model[t, p]
+            for o in range(1, g):
+                total = total + model_r[t, o - 1, p]
+            value = obs_v[i] - total
+            if t == ITERS - 1:
+                res[i] = value
+            resid = components(value)
+            gl = product(resid, components(left_t[i]), adjoint_b=True)
+            gt = product(resid, components(right_t[i]), adjoint_a=True)
+            both = jnp.concatenate(
+                [jnp.concatenate(flat(gl), axis=0), jnp.concatenate(flat(gt), axis=0)], axis=1
+            )
+            acc[...] += lax.dot_general(
+                split_rows(both), onehot[i], (((1,), (1,)), ((), ())),
+                preferred_element_type=jnp.float32,
+            )
+            return 0
+
+        def finish(q):
+            for o in range(1, g):
+                wait_bytes(model_r.at[t, o - 1, pl.ds(q * cg, cg)], m_recv.at[t, o - 1, q])
+            lax.fori_loop(q * cg, (q + 1) * cg, backward, 0)
+
         for q in range(groups):
             lax.fori_loop(q * cg, (q + 1) * cg, forward, 0)
             send_models(q)
+            if t == 0 and q > 0:
+                finish(q - 1)
 
         if t > 0:
             u = t - 1
@@ -244,40 +307,18 @@
                     for m in range(1, 4):
                         value = value + float(basis[f, m]) * coefficients[m]
                     z_send[u, f] = value
-                for f in range(N):
-                    @pl.when(mine != f)
-                    def _():
-                        z_copy(u, f).start()
-
-                    @pl.when(mine == f)
-                    def _():
-                        pltpu.make_async_copy(z_send.at[u, f], z_recv.at[u, f], zr_sem.at[u, f]).start()
-
-        acc[...] = jnp.zeros_like(acc)
-
-        def backward(i, _):
-            total = model[t, i]
-            for o in range(1, g):
-                total = total + model_r[t, o - 1, i]
-            value = obs_v[i] - total
-            if t == ITERS - 1:
-                res[i] = value
-            resid = components(value)
-            gl = product(resid, components(left_t[i]), adjoint_b=True)
-            gt = product(resid, components(right_t[i]), adjoint_a=True)
-            both = jnp.concatenate(
-                [jnp.concatenate(flat(gl), axis=0), jnp.concatenate(flat(gt), axis=0)], axis=1
-            )
-            acc[...] += lax.dot_general(
-                split_rows(both), onehot[i], (((1,), (1,)), ((), ())),
-                preferred_element_type=jnp.float32,
-            )
-            return 0
-
-        for q in range(groups):
-            for o in range(1, g):
-                wait_bytes(model_r.at[t, o - 1, pl.ds(q * cg, cg)], m_recv.at[t, o - 1, q])
-            lax.fori_loop(q * cg, (q + 1) * cg, backward, 0)
+
+                def send_z(o, _):
+                    z_copy(u, (mine + o) % N).start()
+                    return 0
+
+                lax.fori_loop(1, N, send_z, 0)
+                pltpu.make_async_copy(
+                    z_send.at[u, mine], z_recv.at[u, mine], zr_sem.at[u, mine]
+                ).start()
+
+        for q in range(groups - 1 if t == 0 else 0, groups):
+            finish(q)
 
         if t == ITERS - 1:
             def send_res(f, _):
@@ -321,19 +362,31 @@
             for j in range(npc):
                 r0, l0 = (j // lane_parts) * 8, (j % lane_parts) * L
                 t_send[t, j] = target[r0 : r0 + 8, l0 : l0 + L]
-            for j in range(npc):
-                @pl.when(mine != j)
+
+            def send_t(o, _):
+                j = (mine + o) % N
+
+                @pl.when(j < npc)
                 def _():
                     t_copy(t, j).start()
 
-                @pl.when(mine == j)
-                def _():
-                    pltpu.make_async_copy(t_send.at[t, j], t_recv.at[t, j], tr_sem.at[t, j]).start()
+                return 0
+
+            lax.fori_loop(1, N, send_t, 0)
+
+            @pl.when(mine < npc)
+            def _():
+                pltpu.make_async_copy(
+                    t_send.at[t, mine], t_recv.at[t, mine], tr_sem.at[t, mine]
+                ).start()
 
     final = jnp.dot(from_major, jones[...], precision=HIGHEST, preferred_element_type=jnp.float32)
     for d in range(nb):
-        j_send[d] = final[:, d * So : (d + 1) * So].reshape(Kg, 8, So)
-    place = out_j.at[s, pl.ds(r * Kg, Kg)]
+        for q in range(fold):
+            j_send[d, :, q * So : (q + 1) * So] = final[
+                q * short : (q + 1) * short, d * So : (d + 1) * So
+            ]
+    place = out_p.at[me]
     pltpu.make_async_copy(j_send.at[me], place, o_recv.at[1]).start()
 
     def send_jones(o, _):
@@ -388,24 +441,27 @@
     npc = Kg * lane_parts
     L = S // lane_parts
     groups = 4
+    fold = min(128 // So, Kg)
     gp = max(g - 1, 1)
-    cfg = (nb, nband, F, g, K, Kg, So, S, Bo, step, penalty, npc, lane_parts, groups)
+    cfg = (nb, nband, F, g, K, Kg, So, S, Bo, step, penalty, npc, lane_parts, groups, fold)
     f32, bf16, i32 = jnp.float32, jnp.bfloat16, jnp.int32
     V, D = pltpu.VMEM, pltpu.SemaphoreType.DMA
     anywhere = pl.BlockSpec(memory_space=pl.ANY)
-    return tuple(
+    packed, residual = (
         pl.pallas_call(
             functools.partial(kernel, cfg),
             out_shape=(
-                jax.ShapeDtypeStruct((F, K, 8, So), f32),
+                jax.ShapeDtypeStruct((nb, rows // fold, fold * So), f32),
                 jax.ShapeDtypeStruct((F, 8, Bo), f32),
             ),
             in_specs=[anywhere] * 5,
             out_specs=(anywhere, anywhere),
             scratch_shapes=[
+                V((F, K, 8, So), f32),
+                V((nb, rows // fold, fold * So), f32),
                 V((nb, 1, Bo), i32),
                 V((nb, 1, Bo), i32),
-                V((nb, Kg, 8, So), f32),
+                V((nb, rows // fold, fold * So), f32),
                 V((nb, 8, Bo), f32),
                 V((nb, Kg, 8, Bo), f32),
                 V((nb, S, 2 * Bo), bf16),
@@ -424,7 +480,8 @@
                 V((ITERS - 1, N, 8, L), f32),
                 V((ITERS - 1, npc, 8, L), f32),
                 V((nb, 8, Bo), f32),
-                V((nb, Kg, 8, So), f32),
+                V((nb, rows // fold, fold * So), f32),
+                D,
                 D((4,)),
                 D((4,)),
                 D,
@@ -446,6 +503,17 @@
             antenna_first.reshape(1, Bo), antenna_second.reshape(1, Bo),
         )
     )
+    return tuple(
+        pl.pallas_call(
+            functools.partial(unpack_kernel, (nb, g, Kg, So, fold)),
+            out_shape=(
+                jax.ShapeDtypeStruct((F, K, 8, So), f32),
+                jax.ShapeDtypeStruct((F, 8, Bo), f32),
+            ),
+            in_specs=[pl.BlockSpec(memory_space=V)] * 2,
+            out_specs=[pl.BlockSpec(memory_space=V)] * 2,
+        )(packed, residual)
+    )
 
 
 def solution(mesh):

time: 91.9 us -> 75.3 us (0.82)
  Pallas kernels: 88.2 us -> 74.5 us
  local copies, waits for them, and re-layouts: 2.54 us -> 0 us
    pallas_call x1, Pallas kernels: 88.2 us -> 72.6 us  [per_device(): pl.pallas_call(functools.partial(kernel, cfg), out_shape=(jax.ShapeDtypeS...]
    unnamed x4 -> x0, local copies, waits for them, and re-layouts: 2.54 us -> none
    pallas_call x0 -> x1, Pallas kernels: none -> 1.87 us  [per_device(): pl.pallas_call(functools.partial(unpack_kernel, (nb, g, Kg, So, fold)), o...]
where the time goes in v2:
time: 75.3 us; the launch traced here: 75.1 us
  Pallas kernels  74.5 us (99%)
    pallas_call x1, Pallas kernels, per_device(): pl.pallas_call(functools.partial(kernel, cfg), out_shape=(jax.ShapeDtypeS...  72.6 us
    pallas_call x1, Pallas kernels, per_device(): pl.pallas_call(functools.partial(unpack_kernel, (nb, g, Kg, So, fold)), o...  1.87 us

profile of v2, /device:TPU:0, one launch (start us, length us, event | category | flops | bytes accessed | tf_op | source)
XLA Modules:
  0.0 75.1 jit_solution(14178442339689550618)
XLA Ops:
  0.6 72.6 %shard_map.68 = (f32[16,16,128]{2,1,0:T(8,128)}, f32[8,8,256]{2,1,0:T(8,128)}) custom-call(f32[8,16,8,256]{3,2,1,0:T(8,128)} %coh.1, f32[8,8,256]{2,1,0:T(8,128)} %obs.1, f32[8,16,8,32]{3,2,1,0:T(8,128)} %dev.1, s32[1,256]{1,0:T(1,128)} %bitcast.2, s32[1,256]{1,0:T(1,128)} %bitcast.3), custom_call_target="tpu_custom_call" | custom-call | tf_op jit(solution)/shard_map/pallas_call | solution.py:451
  73.3 1.9 %shard_map.69 = (f32[8,16,8,32]{3,2,1,0:T(8,128)}, f32[8,8,256]{2,1,0:T(8,128)}) custom-call(f32[16,16,128]{2,1,0:T(8,128)} %get-tuple-element.4.packed, f32[8,8,256]{2,1,0:T(8,128)} %get-tuple-element.5.residual_in), custom_call_target="tpu_custom_call" | custom-call | tf_op jit(solution)/shard_map/pallas_call | solution.py:507

commit v3 on v2

--- a/solution.py
+++ b/solution.py
@@ -99,6 +99,7 @@
     r = me % g
     mine = mb * F + s
     cg = nb // groups
+    unroll = 2
     load_dev = pltpu.make_async_copy(dev, dev_in, dev_sem)
     load_dev.start()
 
@@ -230,61 +231,68 @@
                     device_id={"base": s * g + d}, device_id_type=MESH,
                 ).start()
 
-        def forward(p, _):
-            i = chunk(p)
-            if t == 0:
-                wait_bytes(coh_v.at[i], coh_recv.at[i])
-                sky_rows = jnp.dot(
-                    to_major, coh_v[i].reshape(rows, Bo), precision=HIGHEST,
+        def forward(step_at, _):
+            at = [step_at * unroll + n for n in range(unroll)]
+            both, skies = [], []
+            for p in at:
+                i = chunk(p)
+                if t == 0:
+                    wait_bytes(coh_v.at[i], coh_recv.at[i])
+                    cohc[p] = jnp.dot(
+                        to_major, coh_v[i].reshape(rows, Bo), precision=HIGHEST,
+                        preferred_element_type=jnp.float32,
+                    )
+                skies.append(cohc[p])
+                both.append(jnp.dot(jj[...], onehot[i], preferred_element_type=jnp.float32))
+            for p, pair, sky_rows in zip(at, both, skies):
+                pair = pair[0:rows] + pair[rows:]
+                sky = components(sky_rows)
+                leading = components(pair[:, 0:Bo])
+                trailing = components(pair[:, Bo:])
+                m = product(sky, trailing, adjoint_b=True)
+                a = product(leading, sky)
+                v = product(leading, m)
+                left_t[p] = jnp.concatenate(flat(m), axis=0)
+                right_t[p] = jnp.concatenate(flat(a), axis=0)
+                model[t, p] = jnp.concatenate(
+                    [jnp.sum(x, axis=0, keepdims=True) for x in flat(v)], axis=0
+                )
+            return 0
+
+        acc[...] = jnp.zeros_like(acc)
+
+        def backward(step_at, _):
+            update = None
+            for n in range(unroll):
+                p = step_at * unroll + n
+                i = chunk(p)
+                total = model[t, p]
+                for o in range(1, g):
+                    total = total + model_r[t, o - 1, p]
+                value = obs_v[i] - total
+                if t == ITERS - 1:
+                    res[i] = value
+                resid = components(value)
+                gl = product(resid, components(left_t[p]), adjoint_b=True)
+                gt = product(resid, components(right_t[p]), adjoint_a=True)
+                both = jnp.concatenate(
+                    [jnp.concatenate(flat(gl), axis=0), jnp.concatenate(flat(gt), axis=0)], axis=1
+                )
+                part = lax.dot_general(
+                    split_rows(both), onehot[i], (((1,), (1,)), ((), ())),
                     preferred_element_type=jnp.float32,
                 )
-                cohc[i] = sky_rows
-            else:
-                sky_rows = cohc[i]
-            both = jnp.dot(jj[...], onehot[i], preferred_element_type=jnp.float32)
-            both = both[0:rows] + both[rows:]
-            sky = components(sky_rows)
-            leading = components(both[:, 0:Bo])
-            trailing = components(both[:, Bo:])
-            m = product(sky, trailing, adjoint_b=True)
-            a = product(leading, sky)
-            v = product(leading, m)
-            left_t[i] = jnp.concatenate(flat(m), axis=0)
-            right_t[i] = jnp.concatenate(flat(a), axis=0)
-            model[t, p] = jnp.concatenate(
-                [jnp.sum(x, axis=0, keepdims=True) for x in flat(v)], axis=0
-            )
-            return 0
-
-        acc[...] = jnp.zeros_like(acc)
-
-        def backward(p, _):
-            i = chunk(p)
-            total = model[t, p]
-            for o in range(1, g):
-                total = total + model_r[t, o - 1, p]
-            value = obs_v[i] - total
-            if t == ITERS - 1:
-                res[i] = value
-            resid = components(value)
-            gl = product(resid, components(left_t[i]), adjoint_b=True)
-            gt = product(resid, components(right_t[i]), adjoint_a=True)
-            both = jnp.concatenate(
-                [jnp.concatenate(flat(gl), axis=0), jnp.concatenate(flat(gt), axis=0)], axis=1
-            )
-            acc[...] += lax.dot_general(
-                split_rows(both), onehot[i], (((1,), (1,)), ((), ())),
-                preferred_element_type=jnp.float32,
-            )
+                update = part if update is None else update + part
+            acc[...] += update
             return 0
 
         def finish(q):
             for o in range(1, g):
                 wait_bytes(model_r.at[t, o - 1, pl.ds(q * cg, cg)], m_recv.at[t, o - 1, q])
-            lax.fori_loop(q * cg, (q + 1) * cg, backward, 0)
+            lax.fori_loop(q * cg // unroll, (q + 1) * cg // unroll, backward, 0)
 
         for q in range(groups):
-            lax.fori_loop(q * cg, (q + 1) * cg, forward, 0)
+            lax.fori_loop(q * cg // unroll, (q + 1) * cg // unroll, forward, 0)
             send_models(q)
             if t == 0 and q > 0:
                 finish(q - 1)

time: 75.3 us -> 72.7 us (0.965)
  Pallas kernels: 74.5 us -> 71.9 us
    pallas_call x1, Pallas kernels: 72.6 us -> 70 us  [per_device(): pl.pallas_call(functools.partial(kernel, cfg), out_shape=(jax.ShapeDtypeS...]
where the time goes in v3:
time: 72.7 us; the launch traced here: 72.5 us
  Pallas kernels  71.9 us (99%)
    pallas_call x1, Pallas kernels, per_device(): pl.pallas_call(functools.partial(kernel, cfg), out_shape=(jax.ShapeDtypeS...  70 us
    pallas_call x1, Pallas kernels, per_device(): pl.pallas_call(functools.partial(unpack_kernel, (nb, g, Kg, So, fold)), o...  1.87 us

profile of v3, /device:TPU:0, one launch (start us, length us, event | category | flops | bytes accessed | tf_op | source)
XLA Modules:
  0.0 72.5 jit_solution(15392943834429728411)
XLA Ops:
  0.6 70.0 %shard_map.68 = (f32[16,16,128]{2,1,0:T(8,128)}, f32[8,8,256]{2,1,0:T(8,128)}) custom-call(f32[8,16,8,256]{3,2,1,0:T(8,128)} %coh.1, f32[8,8,256]{2,1,0:T(8,128)} %obs.1, f32[8,16,8,32]{3,2,1,0:T(8,128)} %dev.1, s32[1,256]{1,0:T(1,128)} %bitcast.2, s32[1,256]{1,0:T(1,128)} %bitcast.3), custom_call_target="tpu_custom_call" | custom-call | tf_op jit(solution)/shard_map/pallas_call | solution.py:459
  70.6 1.9 %shard_map.69 = (f32[8,16,8,32]{3,2,1,0:T(8,128)}, f32[8,8,256]{2,1,0:T(8,128)}) custom-call(f32[16,16,128]{2,1,0:T(8,128)} %get-tuple-element.4.packed, f32[8,8,256]{2,1,0:T(8,128)} %get-tuple-element.5.residual_in), custom_call_target="tpu_custom_call" | custom-call | tf_op jit(solution)/shard_map/pallas_call | solution.py:515
